TPU v7x, 32 devices: a whole 2x2x4 slice. The times are simulated.
32 devices in a mesh: dp: 8 (over y, x, core), seq: 4 (over z).
Axes of the slice: x: 2, y: 2, z: 4, core: 2. Of those that a mesh axis runs over, the one named last changes fastest.
Arguments:
- hidden: bfloat16 [8192, 1792], P(('dp', 'seq')), may hold values from -12.75 to 12.75
- depths: int32 [8192], P(('dp', 'seq')), may hold values from 1 to 3, as said below
- packed_slot_index: int32 [8192], P(('dp', 'seq')), may hold values from -1 to 511, as said below
- value_weight: bfloat16 [1792, 1024], P('dp'), may hold values from -0.125 to 0.125
- output_weight: bfloat16 [1024, 1792], P('dp'), may hold values from -0.1875 to 0.1875
- adapter_down_factor: bfloat16 [1792, 128], P('dp'), may hold values from -0.125 to 0.125
- adapter_up_factor: bfloat16 [1024, 128], P('dp'), may hold values from -0.5 to 0.5
- before_norm_gain: float32 [1792], replicated, may hold values from 0.1 to 1.9
- after_norm_gain: float32 [1792], replicated, may hold values from 0.1 to 1.9
- cotangent: bfloat16 [4096, 1792], P(('dp', 'seq')), may hold values from -6 to 6
Outputs:
- looped: bfloat16 [4096, 1792], P(('dp', 'seq'))
- grad_hidden: bfloat16 [8192, 1792], P(('dp', 'seq'))
- down_factor_gradient: float32 [1792, 128], P('dp', 'seq')
- up_factor_gradient: float32 [1024, 128], P('dp', 'seq')
Inputs may be any that keep to these rules, and one draw needn't show every extreme that they name: `depths`: of the 1024 tokens of one dp index exactly 512 have depth 2 or 3, and all 256 tokens of one seq index are among them. -1 exactly where depths is 1. Over the tokens of one dp index with depth 2 or 3 the slots are a permutation of 0 to 511; packed_slot_index // 128 is the seq index that holds the token's packed row. At most 64 tokens of one device have slots of one seq index, and exactly 64 do in every dp index.
All inputs are finite; a program needn't handle non-finite values.
Results may differ from a plain program's by a relative error of at most 0.01.
Values may be sent and summed in bfloat16 or wider, within the bound.
A program may use at most 64 MiB of HBM per device.

v0:
```python
import math
import jax
import jax.numpy as jnp
from jax import lax
from jax.sharding import PartitionSpec as P

epsilon = 1e-06


def contract_final_axis(left, right):
    return lax.dot_general(
        left, right, (((1,), (1,)), ((), ())), preferred_element_type=jnp.float32
    )


def contract_first(left, right):
    return lax.dot_general(
        left, right, (((0,), (0,)), ((), ())), preferred_element_type=jnp.float32
    )


def layer_forward(
    input_rows,
    cotangent_rows,
    value_weight,
    output_weight,
    adapter_down_factor,
    adapter_up_factor,
    before_norm_gain,
    after_norm_gain,
):
    x_float = input_rows.astype(jnp.float32)
    inv_pre = lax.rsqrt(jnp.mean(x_float * x_float, axis=-1, keepdims=True) + epsilon)
    whitened = x_float * inv_pre
    normalized_rows = (whitened * before_norm_gain).astype(jnp.bfloat16)
    rank_reduced = jnp.dot(
        normalized_rows, adapter_down_factor, preferred_element_type=jnp.float32
    ).astype(jnp.bfloat16)
    projected_rows = (
        jnp.dot(normalized_rows, value_weight, preferred_element_type=jnp.float32)
        + contract_final_axis(rank_reduced, adapter_up_factor)
    ).astype(jnp.bfloat16)
    mixed_out = jnp.dot(projected_rows, output_weight, preferred_element_type=jnp.float32)
    inv_post = lax.rsqrt(jnp.mean(mixed_out * mixed_out, axis=-1, keepdims=True) + epsilon)
    shaped = mixed_out * inv_post
    looped = (x_float + shaped * after_norm_gain).astype(jnp.bfloat16)
    cot_float = cotangent_rows.astype(jnp.float32)
    grad_shaped = cot_float * after_norm_gain
    grad_mixed = (
        inv_post * (grad_shaped - shaped * jnp.mean(grad_shaped * shaped, axis=-1, keepdims=True))
    ).astype(jnp.bfloat16)
    value_gradient = contract_final_axis(grad_mixed, output_weight).astype(jnp.bfloat16)
    low_rank_gradient = jnp.dot(
        value_gradient, adapter_up_factor, preferred_element_type=jnp.float32
    ).astype(jnp.bfloat16)
    normalized_gradient = contract_final_axis(value_gradient, value_weight) + contract_final_axis(
        low_rank_gradient, adapter_down_factor
    )
    grad_white = normalized_gradient * before_norm_gain
    gradient_rows = (
        cot_float
        + inv_pre
        * (grad_white - whitened * jnp.mean(grad_white * whitened, axis=-1, keepdims=True))
    ).astype(jnp.bfloat16)
    down_factor_gradient = contract_first(normalized_rows, low_rank_gradient)
    up_factor_gradient = contract_first(value_gradient, rank_reduced)
    return (looped, gradient_rows, down_factor_gradient, up_factor_gradient)


def body(
    hidden,
    depths,
    packed_slot_index,
    value_weight,
    output_weight,
    adapter_down_factor,
    adapter_up_factor,
    before_norm_gain,
    after_norm_gain,
    cotangent,
):
    seq_count = lax.axis_size("seq")
    own_index = lax.axis_index("seq")
    tok_count = hidden.shape[0]
    act_rows = cotangent.shape[0]
    value_full, out_full, down_full, up_full = (
        lax.all_gather(value_weight, "dp", axis=0, tiled=True),
        lax.all_gather(output_weight, "dp", axis=0, tiled=True),
        lax.all_gather(adapter_down_factor, "dp", axis=0, tiled=True),
        lax.all_gather(adapter_up_factor, "dp", axis=0, tiled=True),
    )
    depth_all, slot_all = (
        lax.all_gather(depths, "seq", axis=0, tiled=True),
        lax.all_gather(packed_slot_index, "seq", axis=0, tiled=True),
    )
    active_all = depth_all >= 2
    dest_all = jnp.where(active_all, slot_all // act_rows, -1)
    pos_all = jnp.where(active_all, slot_all % act_rows, 0)
    mine = active_all & (dest_all == own_index)
    active = depths >= 2
    zero_row = jnp.zeros((), jnp.bfloat16)
    rows_all = lax.all_gather(hidden, "seq", axis=0, tiled=True)
    source = (
        jnp.zeros((act_rows,), jnp.int32)
        .at[jnp.where(mine, pos_all, act_rows)]
        .set(jnp.arange(seq_count * tok_count, dtype=jnp.int32), mode="drop")
    )
    packed = jnp.take(rows_all, source, axis=0)
    looped, gradient_rows, down_factor_gradient, up_factor_gradient = layer_forward(
        packed,
        cotangent,
        value_full,
        out_full,
        down_full,
        up_full,
        before_norm_gain,
        after_norm_gain,
    )
    grads_all = lax.all_gather(gradient_rows, "seq", axis=0, tiled=True)
    picked = jnp.take(grads_all, jnp.maximum(packed_slot_index, 0), axis=0)
    grad_hidden = jnp.where(active[:, None], picked, zero_row)
    grad_scale = 1.0 / math.sqrt(seq_count * act_rows * lax.axis_size("dp"))
    down_term = down_factor_gradient * grad_scale
    up_term = up_factor_gradient * grad_scale
    down_mid, up_mid = (
        lax.psum_scatter(
            down_term.astype(jnp.bfloat16), "seq", scatter_dimension=1, tiled=True
        ).astype(jnp.float32),
        lax.psum_scatter(
            up_term.astype(jnp.bfloat16), "seq", scatter_dimension=1, tiled=True
        ).astype(jnp.float32),
    )
    down_sum, up_sum = (
        lax.psum_scatter(down_mid, "dp", scatter_dimension=0, tiled=True),
        lax.psum_scatter(up_mid, "dp", scatter_dimension=0, tiled=True),
    )
    return (looped, grad_hidden, down_sum, up_sum)


def solution(mesh):
    placed = (
        P(("dp", "seq"), None),
        P(("dp", "seq")),
        P(("dp", "seq")),
        P("dp", None),
        P("dp", None),
        P("dp", None),
        P("dp", None),
        P(),
        P(),
        P(("dp", "seq"), None),
    )
    return jax.shard_map(
        body,
        mesh=mesh,
        in_specs=placed,
        out_specs=(P(("dp", "seq"), None), P(("dp", "seq"), None), P("dp", "seq"), P("dp", "seq")),
        check_vma=False,
    )
```

profile of v0, /device:TPU:0, one launch (start us, length us, event | category | flops | bytes accessed | tf_op | source)
XLA Modules:
  0.0 329.3 jit_solution(13722843027043391828)
XLA Ops:
  7.2 0.0 copy-start.2
  7.2 0.0 all-gather.7.cloned.1.call-start
  7.2 0.7 all-gather.7.cloned.1.call-update
  7.9 0.0 all-gather.9.cloned.1.call-start
  8.0 0.7 all-gather.9.cloned.1.call-update
  8.7 0.0 all-gather.11.cloned.1.call-start
  8.7 0.7 all-gather.11.cloned.1.call-update
  9.4 0.0 reduce-scatter.7.cloned.1.call-start
  9.4 12.8 %all-gather = s32[4,1,256]{2,1,0:T(1,128)S(1)} all-gather(s32[1,1,256]{2,1,0:T(1,128)} %bitcast.21), channel_id=1, replica_groups=mesh['dp'=8,'seq'=4] {'seq'}, dimensions={0}, use_global_device_ids=true | all-gather | bytes 5120 | tf_op jit(solution)/shard_map/all_gather | solution.py:93
  22.3 8.1 %all-gather.1 = s32[4,1,256]{2,1,0:T(1,128)S(1)} all-gather(s32[1,1,256]{2,1,0:T(1,128)} %bitcast.20), channel_id=1, replica_groups=mesh['dp'=8,'seq'=4] {'seq'}, dimensions={0}, use_global_device_ids=true | all-gather | bytes 5120 | tf_op jit(solution)/shard_map/all_gather | solution.py:94
  30.4 4.3 %scatter_custom_fusion = s32[128]{0:T(128)S(1)} fusion(s32[1024]{0:T(1024)S(1)} %compare_select_fusion, s32[1024]{0:T(1024)S(1)} %iota.3, s32[]{:T(128)} %constant.69.clone.1), kind=kCustom, calls=%fused_computation.69 | custom fusion | bytes 516 | tf_op jit(solution)/shard_map/scatter | solution.py:106
  34.8 9.5 %all_gather.29 = bf16[1024,128]{1,0:T(8,128)(2,1)S(1)} all-gather(bf16[128,128]{1,0:T(8,128)(2,1)} %param.16), channel_id=1, replica_groups=mesh['dp'=8,'seq'=4] {'dp'}, dimensions={0}, use_global_device_ids=true | all-gather | bytes 294912 | tf_op jit(solution)/shard_map/all_gather | solution.py:90
  44.3 9.5 %all_gather.28 = bf16[1792,128]{1,0:T(8,128)(2,1)S(1)} all-gather(bf16[224,128]{1,0:T(8,128)(2,1)} %param.15), channel_id=1, replica_groups=mesh['dp'=8,'seq'=4] {'dp'}, dimensions={0}, use_global_device_ids=true | all-gather | bytes 516096 | tf_op jit(solution)/shard_map/all_gather | solution.py:89
  53.8 30.7 %all-gather.7.cloned.1.call-done = bf16[1024,1792]{1,0:T(8,128)(2,1)} async-done(((bf16[256,1792]{1,0:T(8,128)(2,1)}), bf16[1024,1792]{1,0:T(8,128)(2,1)}) %all-gather.7.cloned.1.call-update) | async-done | bytes 3670032 | tf_op jit(solution)/shard_map/all_gather | solution.py:102
  84.5 3.8 %gather_fusion = bf16[128,1792]{1,0:T(8,128)(2,1)S(1)} fusion(bf16[1024,1792]{1,0:T(8,128)(2,1)} %all-gather.7.cloned.1.call-done, s32[1024]{0:T(1024)S(1)} %pad_clamp_fusion.1), kind=kCustom, calls=%fused_computation | custom fusion | bytes 918016 | tf_op jit(solution)/shard_map/jit(_take)/gather | solution.py:108
  88.4 0.3 fusion.18
  88.7 0.0 copy-done.2
  88.7 0.4 convolution_convert_fusion.1
  89.0 30.5 %all-gather.9.cloned.1.call-done = bf16[1792,1024]{1,0:T(8,128)(2,1)} async-done(((bf16[224,1024]{1,0:T(8,128)(2,1)}), bf16[1792,1024]{1,0:T(8,128)(2,1)}) %all-gather.9.cloned.1.call-update) | async-done | bytes 3670032 | tf_op jit(solution)/shard_map/all_gather | solution.py:87
  119.5 2.7 fusion.37
  122.3 0.0 copy-start
  122.3 0.0 copy-start.1
  122.3 33.7 %all-gather.11.cloned.1.call-done = bf16[1024,1792]{1,0:T(8,128)(2,1)} async-done(((bf16[128,1792]{1,0:T(8,128)(2,1)}), bf16[1024,1792]{1,0:T(8,128)(2,1)}) %all-gather.11.cloned.1.call-update) | async-done | bytes 3670032 | tf_op jit(solution)/shard_map/all_gather | solution.py:88
  156.0 2.9 multiply_reduce_fusion
  158.9 0.0 copy-done
  158.9 0.0 copy-done.1
  158.9 1.1 fusion.10
  160.0 3.4 %convolution_convert_fusion = bf16[128,1024]{1,0:T(8,128)(2,1)S(1)} fusion(bf16[1024,1792]{1,0:T(8,128)(2,1)} %all-gather.11.cloned.1.call-done, bf16[128,1792]{1,0:T(8,128)(2,1)S(1)} %copy-done, f32[128,1792]{1,0:T(8,128)S(1)} %get-tuple-element.7, f32[128]{0:T(128)S(1)} %broadcast_multiply_fusion.1, f32[1792]{0:T(1024)S(1)} %copy-done.1, ...), kind=kOutput, calls=%fused_computation.15 | convolution fusion | flops 471498752 | bytes 5316608 | tf_op jit(solution)/shard_map/dot_general | solution.py:11
  163.4 0.2 convolution_convert_fusion.2
  163.6 1.2 fusion.1
  164.8 0.0 reduce-scatter.7.cloned.1.call-update
  164.8 0.0 reduce-scatter.9.cloned.1.call-start
  164.9 1.0 fusion.6
  165.8 0.0 reduce-scatter.9.cloned.1.call-update
  165.8 0.0 reduce-scatter.13.cloned.1.call-start
  165.9 3.4 %fusion.39 = f32[128,1792]{1,0:T(8,128)S(1)} fusion(bf16[128,1024]{1,0:T(8,128)(2,1)S(1)} %convolution_convert_fusion, bf16[1792,1024]{1,0:T(8,128)(2,1)} %all-gather.9.cloned.1.call-done), kind=kOutput, calls=%fused_computation.72 | convolution fusion | flops 469762048 | bytes 4849664 | tf_op jit(solution)/shard_map/dot_general | solution.py:11
  169.3 0.0 copy-start.3
  169.3 0.0 copy-start.4
  169.3 0.4 fusion.15
  169.8 16.2 %reduce-scatter.7.cloned.1.call-done = bf16[1792,32]{0,1:T(8,128)(2,1)} async-done(((bf16[1792,128]{0,1:T(8,128)(2,1)}), bf16[1792,32]{0,1:T(8,128)(2,1)}) %reduce-scatter.7.cloned.1.call-update) | async-done | bytes 114704 | tf_op jit(solution)/shard_map/reduce_scatter | solution.py:126
  186.0 2.0 copy.14
  188.0 0.0 reduce-scatter.13.cloned.1.call-update
  188.0 0.0 all-gather.13.cloned.1.call-start
  188.1 1.3 fusion.13
  189.4 0.0 all-gather.13.cloned.1.call-update
  189.4 0.0 reduce-scatter.11.cloned.1.call-start
  189.5 0.0 copy-done.3
  189.5 0.0 copy-done.4
  189.6 16.7 %reduce-scatter.9.cloned.1.call-done = bf16[1024,32]{0,1:T(8,128)(2,1)} async-done(((bf16[1024,128]{0,1:T(8,128)(2,1)}), bf16[1024,32]{0,1:T(8,128)(2,1)}) %reduce-scatter.9.cloned.1.call-update) | async-done | bytes 65552 | tf_op jit(solution)/shard_map/reduce_scatter | solution.py:129
  206.3 1.5 convert_element_type.55
  207.8 0.0 reduce-scatter.11.cloned.1.call-update
  207.8 35.8 %reduce-scatter.13.cloned.1.call-done = f32[224,32]{1,0:T(8,128)} async-done(((f32[1792,32]{1,0:T(8,128)}), f32[224,32]{1,0:T(8,128)}) %reduce-scatter.13.cloned.1.call-update) | async-done | bytes 28688
  243.6 1.6 copy.15
  245.2 41.4 %all-gather.13.cloned.1.call-done = bf16[512,1792]{1,0:T(8,128)(2,1)} async-done(((bf16[128,1792]{1,0:T(8,128)(2,1)}), bf16[512,1792]{1,0:T(8,128)(2,1)}) %all-gather.13.cloned.1.call-update) | async-done | bytes 1835024 | tf_op jit(solution)/shard_map/all_gather | solution.py:119
  286.6 3.9 %gather_fusion.1 = bf16[256,1792]{1,0:T(8,128)(2,1)S(1)} fusion(bf16[512,1792]{1,0:T(8,128)(2,1)} %all-gather.13.cloned.1.call-done, s32[1024]{0:T(1024)S(1)} %pad_clamp_fusion), kind=kCustom, calls=%fused_computation.1 | custom fusion | bytes 1836032 | tf_op jit(solution)/shard_map/jit(_take)/gather | solution.py:120
  290.5 1.1 select_select_fusion
  291.6 30.8 %reduce-scatter.11.cloned.1.call-done = f32[128,32]{0,1:T(8,128)} async-done(((f32[1024,32]{0,1:T(8,128)}), f32[128,32]{0,1:T(8,128)}) %reduce-scatter.11.cloned.1.call-update) | async-done | bytes 16400 | tf_op jit(solution)/shard_map/reduce_scatter | solution.py:135
  (15 shorter events, 0.1 us)
Async XLA Ops:
  7.2 81.5 %copy-start.2 = (f32[1792]{0:T(1024)S(1)}, f32[1792]{0:T(1024)}, u32[]{:S(2)}) copy-start(f32[1792]{0:T(1024)} %param.17) | copy-start | bytes 21508
  7.2 77.3 %all-gather.7.cloned.1.call-start = ((), (), s32[]{:S(2)}) async-start(), calls=%async_computation.4 | async-start | bytes 4587520 | tf_op jit(solution)/shard_map/all_gather | solution.py:102
  7.9 111.6 %all-gather.9.cloned.1.call-start = ((), (), s32[]{:S(2)}) async-start(), calls=%async_computation.5 | async-start | bytes 4128768 | tf_op jit(solution)/shard_map/all_gather | solution.py:87
  8.7 147.3 %all-gather.11.cloned.1.call-start = ((), (), s32[]{:S(2)}) async-start(), calls=%async_computation.6 | async-start | bytes 4128768 | tf_op jit(solution)/shard_map/all_gather | solution.py:88
  9.4 176.6 %reduce-scatter.7.cloned.1.call-start = ((), (), s32[]{:S(2)}) async-start(), calls=%async_computation.8 | async-start | bytes 573440 | tf_op jit(solution)/shard_map/reduce_scatter | solution.py:126
  122.3 36.7 %copy-start = (bf16[128,1792]{1,0:T(8,128)(2,1)S(1)}, bf16[128,1792]{1,0:T(8,128)(2,1)}, u32[]{:S(2)}) copy-start(bf16[128,1792]{1,0:T(8,128)(2,1)} %param.19) | copy-start | bytes 1376260
  122.3 36.6 %copy-start.1 = (f32[1792]{0:T(1024)S(1)}, f32[1792]{0:T(1024)}, u32[]{:S(2)}) copy-start(f32[1792]{0:T(1024)} %param.18) | copy-start | bytes 21508
  164.8 41.5 %reduce-scatter.9.cloned.1.call-start = ((), (), s32[]{:S(2)}) async-start(), calls=%async_computation.9 | async-start | bytes 327680 | tf_op jit(solution)/shard_map/reduce_scatter | solution.py:129
  165.8 77.8 %reduce-scatter.13.cloned.1.call-start = ((), (), s32[]{:S(2)}) async-start(), calls=%async_computation.11 | async-start | bytes 1032192
  169.3 20.2 %copy-start.3 = (s32[256]{0:T(256)S(1)}, s32[256]{0:T(256)}, u32[]{:S(2)}) copy-start(s32[256]{0:T(256)} %param.12) | copy-start | bytes 3076
  169.3 20.3 %copy-start.4 = (s32[256]{0:T(256)S(1)}, s32[256]{0:T(256)}, u32[]{:S(2)}) copy-start(s32[256]{0:T(256)} %param.11) | copy-start | bytes 3076
  188.0 98.6 %all-gather.13.cloned.1.call-start = ((), (), s32[]{:S(2)}) async-start(), calls=%async_computation.7 | async-start | bytes 2293760 | tf_op jit(solution)/shard_map/all_gather | solution.py:119
  189.4 133.0 %reduce-scatter.11.cloned.1.call-start = ((), (), s32[]{:S(2)}) async-start(), calls=%async_computation.10 | async-start | bytes 147456 | tf_op jit(solution)/shard_map/reduce_scatter | solution.py:135
Sparse Core Ops, SparseCore 0:
  9.6 74.8 all-gather.6
  86.4 33.0 all-gather.8
  121.4 34.5 all-gather.10
  164.9 20.9 reduce-scatter.6
  188.2 18.0 reduce-scatter.8
  209.9 33.6 reduce-scatter.12
  245.2 41.3 all-gather.12
  290.2 32.2 reduce-scatter.10
where the time goes:
time: 330 us; the launch traced here: 329 us
  waiting for transfers between devices  238 us (72%)
  blocking collectives  39.9 us (12%)
  local copies, waits for them, and re-layouts  15.7 us (5%)
  matrix products  15.5 us (5%)
  between operations  14.3 us (4%)
  other arithmetic  5.43 us (2%)
    all_gather x1, waiting for transfers between devices, body(): grads_all = lax.all_gather(gradient_rows, 'seq', axis=0, tiled=True)  41.4 us
    unnamed x9, waiting for transfers between devices  38 us
    all_gather x1, waiting for transfers between devices, body(): lax.all_gather(output_weight, 'dp', axis=0, tiled=True)  33.7 us
    reduce_scatter x1, waiting for transfers between devices, body(): lax.psum_scatter(up_mid, 'dp', scatter_dimension=0, tiled=True)  30.8 us
    all_gather x1, waiting for transfers between devices, body(): rows_all = lax.all_gather(hidden, 'seq', axis=0, tiled=True)  30.7 us
    all_gather x1, waiting for transfers between devices, body(): lax.all_gather(value_weight, 'dp', axis=0, tiled=True)  30.5 us
    reduce_scatter x1, waiting for transfers between devices, body(): lax.psum_scatter(up_term.astype(jnp.bfloat16), 'seq', scatter_dimension=1...  16.7 us
    reduce_scatter x1, waiting for transfers between devices, body(): lax.psum_scatter(down_term.astype(jnp.bfloat16), 'seq', scatter_dimension...  16.2 us
  transfers between devices with their start and end apart: 8, of which 8 were waited for; matrix products, arithmetic and copies ran while one was open for 8% of the time, Pallas kernels for 0%

commit v1 on v0

--- a/solution.py
+++ b/solution.py
@@ -5,6 +5,24 @@
 from jax.sharding import PartitionSpec as P
 
 epsilon = 1e-06
+
+
+def trails_read(original, dim_no):
+    local_next = list(original.shape[1:])
+    local_next[dim_no] *= original.shape[0]
+    return jnp.moveaxis(original, 0, dim_no).reshape(local_next)
+
+
+def note_notes(panel, peer_axis):
+    many = lax.axis_size(peer_axis)
+    u_next = panel[None]
+    for dev_i in range(many.bit_length() - 1):
+        oldest = 1 << dev_i
+        reply = lax.ppermute(u_next, peer_axis, [(c, c ^ oldest) for c in range(many)])
+        carry = jnp.stack([u_next, reply], axis=0)
+        heard = lax.axis_index(peer_axis) >> dev_i & 1
+        u_next = jnp.where(heard == 0, carry, carry[::-1]).reshape(-1, *panel.shape)
+    return u_next
 
 
 def contract_final_axis(left, right):
@@ -83,9 +101,14 @@
     own_index = lax.axis_index("seq")
     tok_count = hidden.shape[0]
     act_rows = cotangent.shape[0]
+
+    def direct_figure_for(xin, chunk, d0):
+        z2 = note_notes(xin, chunk)
+        return trails_read(z2, d0)
+
     value_full, out_full, down_full, up_full = (
         lax.all_gather(value_weight, "dp", axis=0, tiled=True),
-        lax.all_gather(output_weight, "dp", axis=0, tiled=True),
+        direct_figure_for(output_weight, "dp", 0),
         lax.all_gather(adapter_down_factor, "dp", axis=0, tiled=True),
         lax.all_gather(adapter_up_factor, "dp", axis=0, tiled=True),
     )

time: 330 us -> 296 us (0.90)
  waiting for transfers between devices: 238 us -> 183 us
  blocking collectives: 39.9 us -> 49.7 us
  other arithmetic: 5.43 us -> 11.7 us
  starting transfers between devices: 0.32 us -> 5.56 us
    all_gather x1 -> x0, waiting for transfers between devices: 33.7 us -> none  [body(): lax.all_gather(output_weight, 'dp', axis=0, tiled=True)]
    all_gather x1, waiting for transfers between devices: 30.7 us -> 0.01 us  [body(): rows_all = lax.all_gather(hidden, 'seq', axis=0, tiled=True)]
    ppermute x0 -> x3, waiting for transfers between devices: none -> 22.3 us  [note_notes(): lax.ppermute(u_next, peer_axis, [(c, c ^ oldest) for c in range(many)])]
    all_gather x1, waiting for transfers between devices: 30.5 us -> 18.3 us  [body(): lax.all_gather(value_weight, 'dp', axis=0, tiled=True)]
    all_gather x1, blocking collectives: 9.53 us -> 20.3 us  [body(): lax.all_gather(adapter_up_factor, 'dp', axis=0, tiled=True)]
    ppermute x0 -> x3, starting transfers between devices: none -> 5.28 us  [note_notes(): lax.ppermute(u_next, peer_axis, [(c, c ^ oldest) for c in range(many)])]
    another operation x0 -> x4, other arithmetic: none -> 3.36 us  [note_notes(): carry = jnp.stack([u_next, reply], axis=0)]
    unnamed x9 -> x8, waiting for transfers between devices: 38 us -> 37.3 us
  transfers between devices with their start and end apart: 8 -> 10, of which waited for: 8 -> 8; matrix products, arithmetic and copies ran while one was open for 8% -> 11% of each run, Pallas kernels for 0% -> 0%
where the time goes in v1:
time: 296 us
  waiting for transfers between devices  183 us (62%)
  blocking collectives  49.7 us (17%)
  local copies, waits for them, and re-layouts  15.7 us (5%)
  matrix products  15.6 us (5%)
  between operations  14.3 us (5%)
  other arithmetic  11.7 us (4%)
  starting transfers between devices  5.56 us (2%)
    all_gather x1, waiting for transfers between devices, body(): grads_all = lax.all_gather(gradient_rows, 'seq', axis=0, tiled=True)  41.3 us
    unnamed x8, waiting for transfers between devices  37.3 us
    reduce_scatter x1, waiting for transfers between devices, body(): lax.psum_scatter(up_mid, 'dp', scatter_dimension=0, tiled=True)  30.8 us
    ppermute x3, waiting for transfers between devices, note_notes(): lax.ppermute(u_next, peer_axis, [(c, c ^ oldest) for c in range(many)])  22.3 us
    all_gather x1, blocking collectives, body(): lax.all_gather(adapter_up_factor, 'dp', axis=0, tiled=True)  20.3 us
    all_gather x1, waiting for transfers between devices, body(): lax.all_gather(value_weight, 'dp', axis=0, tiled=True)  18.3 us
    reduce_scatter x1, waiting for transfers between devices, body(): lax.psum_scatter(up_term.astype(jnp.bfloat16), 'seq', scatter_dimension=1...  16.7 us
    reduce_scatter x1, waiting for transfers between devices, body(): lax.psum_scatter(down_term.astype(jnp.bfloat16), 'seq', scatter_dimension...  16.3 us
  transfers between devices with their start and end apart: 10, of which 8 were waited for; matrix products, arithmetic and copies ran while one was open for 11% of the time, Pallas kernels for 0%

profile of v1, /device:TPU:0, one launch (start us, length us, event | category | flops | bytes accessed | tf_op | source)
XLA Modules:
  0.0 295.6 jit_solution(17292823335135200075)
XLA Ops:
  7.2 0.0 all-gather.6.cloned.1.call-start
  7.2 0.7 all-gather.6.cloned.1.call-update
  7.9 0.0 all-gather.8.cloned.1.call-start
  7.9 0.7 all-gather.8.cloned.1.call-update
  8.6 0.0 reduce-scatter.7.cloned.1.call-start
  8.7 0.5 collective-permute-start
  9.2 1.7 collective-permute-done
  10.9 1.1 pad_maximum_fusion.2
  12.0 0.2 fusion.21
  12.1 2.9 collective-permute-start.1
  15.1 20.7 %collective-permute-done.1 = bf16[2,128,1792]{2,1,0:T(8,128)(2,1)S(1)} collective-permute-done((bf16[2,128,1792]{2,1,0:T(8,128)(2,1)S(1)}, bf16[2,128,1792]{2,1,0:T(8,128)(2,1)S(1)}, u32[]{:S(2)}, u32[]{:S(2)}) %collective-permute-start.1) | collective-permute-done | bytes 917536 | tf_op jit(solution)/shard_map/ppermute | solution.py:21
  35.7 0.2 pad_maximum_fusion.1
  35.9 0.3 reverse_select_fusion.1
  36.2 1.8 collective-permute-start.2
  38.1 0.0 copy-done.6
  38.1 11.3 %all-gather = s32[4,1,256]{2,1,0:T(1,128)S(1)} all-gather(s32[1,1,256]{2,1,0:T(1,128)S(1)} %bitcast.41), channel_id=1, replica_groups=mesh['dp'=8,'seq'=4] {'seq'}, dimensions={0}, use_global_device_ids=true | all-gather | bytes 5120 | tf_op jit(solution)/shard_map/all_gather | solution.py:116
  49.4 0.0 copy-done.5
  49.4 8.4 %all-gather.1 = s32[4,1,256]{2,1,0:T(1,128)S(1)} all-gather(s32[1,1,256]{2,1,0:T(1,128)S(1)} %bitcast.40), channel_id=1, replica_groups=mesh['dp'=8,'seq'=4] {'seq'}, dimensions={0}, use_global_device_ids=true | all-gather | bytes 5120 | tf_op jit(solution)/shard_map/all_gather | solution.py:117
  57.9 4.3 %scatter_custom_fusion = s32[128]{0:T(128)S(1)} fusion(s32[1024]{0:T(1024)S(1)} %compare_select_fusion, s32[1024]{0:T(1024)S(1)} %iota.3, s32[]{:T(128)} %constant.74.clone.1), kind=kCustom, calls=%fused_computation.77 | custom fusion | bytes 516 | tf_op jit(solution)/shard_map/scatter | solution.py:129
  62.2 0.0 copy-done.4
  62.2 20.3 %all_gather.26 = bf16[1024,128]{1,0:T(8,128)(2,1)S(1)} all-gather(bf16[128,128]{1,0:T(8,128)(2,1)S(1)} %copy-done.4), channel_id=1, replica_groups=mesh['dp'=8,'seq'=4] {'dp'}, dimensions={0}, use_global_device_ids=true | all-gather | bytes 294912 | tf_op jit(solution)/shard_map/all_gather | solution.py:113
  82.5 0.0 copy-done.1
  82.5 9.7 %all_gather.25 = bf16[1792,128]{1,0:T(8,128)(2,1)S(1)} all-gather(bf16[224,128]{1,0:T(8,128)(2,1)S(1)} %copy-done.1), channel_id=1, replica_groups=mesh['dp'=8,'seq'=4] {'dp'}, dimensions={0}, use_global_device_ids=true | all-gather | bytes 516096 | tf_op jit(solution)/shard_map/all_gather | solution.py:112
  92.2 0.0 collective-permute-done.2
  92.2 1.9 pad_maximum_fusion
  94.1 2.6 reverse_select_fusion
  96.7 3.9 %gather_fusion = bf16[128,1792]{1,0:T(8,128)(2,1)S(1)} fusion(bf16[1024,1792]{1,0:T(8,128)(2,1)} %all-gather.6.cloned.1.call-done, s32[1024]{0:T(1024)S(1)} %pad_clamp_fusion.1), kind=kCustom, calls=%fused_computation | custom fusion | bytes 918016 | tf_op jit(solution)/shard_map/jit(_take)/gather | solution.py:131
  100.6 0.3 fusion.18
  100.9 0.0 copy-done.3
  100.9 0.4 convolution_convert_fusion.1
  101.3 18.3 %all-gather.8.cloned.1.call-done = bf16[1792,1024]{1,0:T(8,128)(2,1)} async-done(((bf16[224,1024]{1,0:T(8,128)(2,1)}), bf16[1792,1024]{1,0:T(8,128)(2,1)}) %all-gather.8.cloned.1.call-update) | async-done | bytes 3670032 | tf_op jit(solution)/shard_map/all_gather | solution.py:110
  119.5 2.7 fusion.39
  122.3 0.0 copy-start
  122.3 0.0 copy-start.2
  122.3 3.0 %multiply_reduce_fusion = (f32[128]{0:T(128)S(1)}, f32[128,1792]{1,0:T(8,128)S(1)}) fusion(bf16[1024,1792]{1,0:T(8,128)(2,1)} %bitcast.31, f32[128,1024]{1,0:T(8,128)S(1)} %fusion.39, bf16[128,128]{1,0:T(8,128)(2,1)S(1)} %convolution_convert_fusion.1, bf16[1024,128]{1,0:T(8,128)(2,1)S(1)} %all_gather.26), kind=kOutput, calls=%fused_computation.42 | convolution fusion | flops 504037248 | bytes 5407232 | tf_op jit(solution)/shard_map/dot_general | solution.py:61
  125.3 0.0 copy-done
  125.3 0.0 copy-done.2
  125.3 1.1 fusion.10
  126.4 3.4 %convolution_convert_fusion = bf16[128,1024]{1,0:T(8,128)(2,1)S(1)} fusion(bf16[1024,1792]{1,0:T(8,128)(2,1)} %bitcast.32, bf16[128,1792]{1,0:T(8,128)(2,1)S(1)} %copy-done, f32[128,1792]{1,0:T(8,128)S(1)} %get-tuple-element.9, f32[128]{0:T(128)S(1)} %broadcast_multiply_fusion.1, f32[1792]{0:T(1024)S(1)} %copy-done.2, f32[128]{0:T(128)S(1)} %add_rsqrt_fusion), kind=kOutput, calls=%fused_computation.20 | convolution fusion | flops 471498752 | bytes 5316608 | tf_op jit(solution)/shard_map/dot_general | solution.py:29
  129.8 0.2 convolution_convert_fusion.2
  130.0 1.2 fusion.1
  131.2 0.0 reduce-scatter.7.cloned.1.call-update
  131.2 0.0 reduce-scatter.9.cloned.1.call-start
  131.2 1.0 fusion.6
  132.2 0.0 reduce-scatter.9.cloned.1.call-update
  132.2 0.0 reduce-scatter.13.cloned.1.call-start
  132.3 3.4 %fusion.41 = f32[128,1792]{1,0:T(8,128)S(1)} fusion(bf16[128,1024]{1,0:T(8,128)(2,1)S(1)} %convolution_convert_fusion, bf16[1792,1024]{1,0:T(8,128)(2,1)} %all-gather.8.cloned.1.call-done), kind=kOutput, calls=%fused_computation.80 | convolution fusion | flops 469762048 | bytes 4849664 | tf_op jit(solution)/shard_map/dot_general | solution.py:29
  135.7 0.4 fusion.15
  136.1 16.3 %reduce-scatter.7.cloned.1.call-done = bf16[1792,32]{0,1:T(8,128)(2,1)} async-done(((bf16[1792,128]{0,1:T(8,128)(2,1)}), bf16[1792,32]{0,1:T(8,128)(2,1)}) %reduce-scatter.7.cloned.1.call-update) | async-done | bytes 114704 | tf_op jit(solution)/shard_map/reduce_scatter | solution.py:149
  152.4 2.0 copy.14
  154.4 0.0 reduce-scatter.13.cloned.1.call-update
  154.4 0.0 all-gather.10.cloned.1.call-start
  154.5 1.3 fusion.13
  155.8 0.0 all-gather.10.cloned.1.call-update
  155.9 0.0 reduce-scatter.11.cloned.1.call-start
  156.0 16.7 %reduce-scatter.9.cloned.1.call-done = bf16[1024,32]{0,1:T(8,128)(2,1)} async-done(((bf16[1024,128]{0,1:T(8,128)(2,1)}), bf16[1024,32]{0,1:T(8,128)(2,1)}) %reduce-scatter.9.cloned.1.call-update) | async-done | bytes 65552 | tf_op jit(solution)/shard_map/reduce_scatter | solution.py:152
  172.7 1.5 convert_element_type.55
  174.2 0.0 reduce-scatter.11.cloned.1.call-update
  174.2 35.8 %reduce-scatter.13.cloned.1.call-done = f32[224,32]{1,0:T(8,128)} async-done(((f32[1792,32]{1,0:T(8,128)}), f32[224,32]{1,0:T(8,128)}) %reduce-scatter.13.cloned.1.call-update) | async-done | bytes 28688
  210.0 1.6 copy.15
  211.6 41.3 %all-gather.10.cloned.1.call-done = bf16[512,1792]{1,0:T(8,128)(2,1)} async-done(((bf16[128,1792]{1,0:T(8,128)(2,1)}), bf16[512,1792]{1,0:T(8,128)(2,1)}) %all-gather.10.cloned.1.call-update) | async-done | bytes 1835024 | tf_op jit(solution)/shard_map/all_gather | solution.py:142
  252.9 3.9 %gather_fusion.1 = bf16[256,1792]{1,0:T(8,128)(2,1)S(1)} fusion(bf16[512,1792]{1,0:T(8,128)(2,1)} %all-gather.10.cloned.1.call-done, s32[1024]{0:T(1024)S(1)} %pad_clamp_fusion), kind=kCustom, calls=%fused_computation.1 | custom fusion | bytes 1836032 | tf_op jit(solution)/shard_map/jit(_take)/gather | solution.py:143
  256.7 1.1 select_select_fusion
  257.9 30.8 %reduce-scatter.11.cloned.1.call-done = f32[128,32]{0,1:T(8,128)} async-done(((f32[1024,32]{0,1:T(8,128)}), f32[128,32]{0,1:T(8,128)}) %reduce-scatter.11.cloned.1.call-update) | async-done | bytes 16400 | tf_op jit(solution)/shard_map/reduce_scatter | solution.py:158
  (21 shorter events, 0.1 us)
Async XLA Ops:
  7.2 89.6 %all-gather.6.cloned.1.call-start = ((), (), s32[]{:S(2)}) async-start(), calls=%async_computation.4 | async-start | bytes 4587520 | tf_op jit(solution)/shard_map/all_gather | solution.py:125
  7.9 111.6 %all-gather.8.cloned.1.call-start = ((), (), s32[]{:S(2)}) async-start(), calls=%async_computation.5 | async-start | bytes 4128768 | tf_op jit(solution)/shard_map/all_gather | solution.py:110
  8.6 143.7 %reduce-scatter.7.cloned.1.call-start = ((), (), s32[]{:S(2)}) async-start(), calls=%async_computation.7 | async-start | bytes 573440 | tf_op jit(solution)/shard_map/reduce_scatter | solution.py:149
  8.7 2.2 collective-permute-start
  12.1 23.6 %collective-permute-start.1 = (bf16[2,128,1792]{2,1,0:T(8,128)(2,1)S(1)}, bf16[2,128,1792]{2,1,0:T(8,128)(2,1)S(1)}, u32[]{:S(2)}, u32[]{:S(2)}) collective-permute-start(bf16[2,128,1792]{2,1,0:T(8,128)(2,1)S(1)} %get-tuple-element.7), channel_id=1, source_target_pairs={{0,8},{4,12},{8,0},{12,4},{16,24},{20,28},{24,16},{28,20},{1,9},{5... | collective-permute-start | bytes 2752520 | tf_op jit(solution)/shard_map/ppermute | solution.py:21
  35.7 2.3 copy-start.6
  35.7 13.7 %copy-start.5 = (s32[256]{0:T(256)S(1)}, s32[256]{0:T(256)}, u32[]{:S(2)}) copy-start(s32[256]{0:T(256)} %param.12) | copy-start | bytes 3076
  35.7 26.5 %copy-start.4 = (bf16[128,128]{1,0:T(8,128)(2,1)S(1)}, bf16[128,128]{1,0:T(8,128)(2,1)}, u32[]{:S(2)}) copy-start(bf16[128,128]{1,0:T(8,128)(2,1)} %param.16) | copy-start | bytes 98308
  35.7 46.8 %copy-start.1 = (bf16[224,128]{1,0:T(8,128)(2,1)S(1)}, bf16[224,128]{1,0:T(8,128)(2,1)}, u32[]{:S(2)}) copy-start(bf16[224,128]{1,0:T(8,128)(2,1)} %param.15) | copy-start | bytes 172036
  36.2 56.0 %collective-permute-start.2 = (bf16[4,128,1792]{2,1,0:T(8,128)(2,1)S(1)}, bf16[4,128,1792]{2,1,0:T(8,128)(2,1)}, u32[]{:S(2)}, u32[]{:S(2)}) collective-permute-start(bf16[4,128,1792]{2,1,0:T(8,128)(2,1)S(1)} %bitcast.33), channel_id=1, source_target_pairs={{0,16},{4,20},{8,24},{12,28},{16,0},{20,4},{24,8},{28,12},{1,17},{... | collective-permute-start | bytes 5505032 | tf_op jit(solution)/shard_map/ppermute | solution.py:21
  96.7 4.2 %copy-start.3 = (f32[1792]{0:T(1024)S(1)}, f32[1792]{0:T(1024)}, u32[]{:S(2)}) copy-start(f32[1792]{0:T(1024)} %param.17) | copy-start | bytes 21508
  122.3 3.0 %copy-start = (bf16[128,1792]{1,0:T(8,128)(2,1)S(1)}, bf16[128,1792]{1,0:T(8,128)(2,1)}, u32[]{:S(2)}) copy-start(bf16[128,1792]{1,0:T(8,128)(2,1)} %param.19) | copy-start | bytes 1376260
  122.3 3.0 %copy-start.2 = (f32[1792]{0:T(1024)S(1)}, f32[1792]{0:T(1024)}, u32[]{:S(2)}) copy-start(f32[1792]{0:T(1024)} %param.18) | copy-start | bytes 21508
  131.2 41.5 %reduce-scatter.9.cloned.1.call-start = ((), (), s32[]{:S(2)}) async-start(), calls=%async_computation.8 | async-start | bytes 327680 | tf_op jit(solution)/shard_map/reduce_scatter | solution.py:152
  132.2 77.8 %reduce-scatter.13.cloned.1.call-start = ((), (), s32[]{:S(2)}) async-start(), calls=%async_computation.10 | async-start | bytes 1032192
  154.4 98.4 %all-gather.10.cloned.1.call-start = ((), (), s32[]{:S(2)}) async-start(), calls=%async_computation.6 | async-start | bytes 2293760 | tf_op jit(solution)/shard_map/all_gather | solution.py:142
  155.9 132.8 %reduce-scatter.11.cloned.1.call-start = ((), (), s32[]{:S(2)}) async-start(), calls=%async_computation.9 | async-start | bytes 147456 | tf_op jit(solution)/shard_map/reduce_scatter | solution.py:158
Sparse Core Ops, SparseCore 0:
  9.6 74.8 all-gather.5
  86.4 33.1 all-gather.7
  131.3 21.0 reduce-scatter.6
  154.6 18.0 reduce-scatter.8
  176.3 33.6 reduce-scatter.12
  211.4 41.3 all-gather.9
  256.4 32.2 reduce-scatter.10
